TPU v7x, 256 devices: a whole 4x4x8 slice. The times are simulated.
256 devices in a mesh: col: 16 (over z, core), row: 16 (over x, y).
Axes of the slice: x: 4, y: 4, z: 8, core: 2. Of those that a mesh axis runs over, the one named last changes fastest.
Arguments:
- lower_cols: float32 [4096, 2048], P('col', 'row'), may hold values from -6 to 6
- pivot_rows: float32 [8192, 4096], P('row', 'col')
- pattern: int32 [64, 32], replicated, may hold values 0 or 1
- panel_in: float32 [8192, 2048], P('col', 'row'), may hold values from -6 to 6
- diag_in: float32 [64, 128, 128], P('col'), as said below
Outputs:
- panel: float32 [8192, 2048], P('col', 'row')
- factor: float32 [64, 128, 128], P('col')
Inputs may be any that keep to these rules, and one draw needn't show every extreme that they name: diag_in holds symmetric blocks with diagonal entries between 2.5 and 4.5; diag_in[j] - dsum[j] is positive definite.
All inputs are finite; a program needn't handle non-finite values.
Results may differ from a plain program's by a relative error of at most 0.00005.
Values sent between devices are 32-bit elements; how exact they have to be, the bound alone decides.
A program may use at most 128 MiB of HBM per device.

v0:
```python
import jax
import jax.numpy as jnp
from jax import lax
from jax.sharding import PartitionSpec as P

B = 128


def shards(lower_cols, pivot_rows, pattern, panel_in, diag_in):
    col_index = lax.axis_index("col")
    k_local = lower_cols.shape[0] // B
    targets = pattern.shape[0]
    own_targets = diag_in.shape[0]
    width = panel_in.shape[1]
    whole_pivot = lax.all_gather(pivot_rows, "row", axis=0, tiled=True)
    local_pattern = lax.dynamic_slice_in_dim(pattern, col_index * k_local, k_local, 1).astype(
        jnp.float32
    )
    masked = whole_pivot.reshape(targets, B, k_local, B) * local_pattern[:, None, :, None]
    masked = masked.reshape(targets * B, k_local * B)
    update = lax.psum_scatter(
        jnp.dot(
            masked, lower_cols, precision=lax.Precision.HIGHEST, preferred_element_type=jnp.float32
        ),
        "col",
        scatter_dimension=0,
        tiled=True,
    )
    blocks = masked.reshape(targets, B, k_local * B)
    partial_diag = jnp.einsum("jak,jbk->jab", blocks, blocks, precision=lax.Precision.HIGHEST)
    dsum = lax.psum_scatter(partial_diag, "col", scatter_dimension=0, tiled=True)
    factor = jnp.linalg.cholesky(diag_in - dsum)
    residue = (panel_in - update).reshape(own_targets, B, width)
    solved = lax.linalg.triangular_solve(factor, residue, left_side=True, lower=True)
    return (solved.reshape(own_targets * B, width), factor)


def solution(mesh):
    in_specs = (P("col", "row"), P("row", "col"), P(), P("col", "row"), P("col", None, None))
    out_specs = (P("col", "row"), P("col", None, None))
    return jax.shard_map(shards, mesh=mesh, in_specs=in_specs, out_specs=out_specs, check_vma=False)
```

profile of v0, /device:TPU:2, one launch (start us, length us, event | category | flops | bytes accessed | tf_op | source)
XLA Modules:
  0.0 266.4 jit_solution(10246708308004626296)
XLA Ops:
  7.2 0.0 copy-start
  7.2 0.0 all-gather.2.cloned.1.call-start
  7.2 0.7 all-gather.2.cloned.1.call-update
  7.9 0.0 reduce-scatter.3.cloned.1.call-start
  8.0 0.7 dynamic-slice_convert_fusion
  8.7 0.1 copy.13
  8.8 0.1 mul.24
  8.9 80.3 %all-gather.2.cloned.1.call-done = f32[8192,256]{1,0:T(8,128)} async-done(((f32[512,256]{1,0:T(8,128)}), f32[8192,256]{1,0:T(8,128)}) %all-gather.2.cloned.1.call-update) | async-done | bytes 8388624 | tf_op jit(solution)/shard_map/all_gather | solution.py:15
  89.2 16.6 %fusion.2 = f32[64,128,128]{1,2,0:T(8,128)} fusion(f32[64,128,256]{2,1,0:T(8,128)} %bitcast.23, f32[64,256]{1,0:T(8,128)S(1)} %bitcast.26), kind=kOutput, calls=%fused_computation.3 | convolution fusion | flops 3223322624 | bytes 12648448 | tf_op jit(solution)/shard_map/jak,jbk->jab/dot_general | solution.py:30
  105.8 0.0 reduce-scatter.3.cloned.1.call-update
  105.9 0.0 reduce-scatter.5.cloned.1.call-start
  105.9 5.4 %mul.28 = f32[64,128,2,128]{3,2,1,0:T(2,128)} broadcast(f32[64,2]{1,0:T(8,128)S(1)} %copy.13), dimensions={0,2} | broadcast | bytes 8389120 | tf_op jit(solution)/shard_map/mul | solution.py:19
  111.3 0.0 copy-done
  111.3 0.0 copy-start.2
  111.3 0.0 copy-start.1
  111.3 12.2 %fusion = f32[8192,128]{1,0:T(8,128)} fusion(f32[256,128]{1,0:T(8,128)S(1)} %copy-done, f32[8192,256]{1,0:T(8,128)} %all-gather.2.cloned.1.call-done, f32[1024,8,2,128]{3,2,1,0:T(2,128)} %bitcast.24), kind=kOutput, calls=%fused_computation.1 | convolution fusion | flops 3223322624 | bytes 21102592 | tf_op jit(solution)/shard_map/dot_general | solution.py:22
  123.5 0.0 reduce-scatter.5.cloned.1.call-update
  123.6 0.0 copy-done.2
  123.6 0.1 copy.15
  123.8 45.4 %reduce-scatter.3.cloned.1.call-done = f32[4,128,128]{1,2,0:T(8,128)} async-done(((f32[64,128,128]{1,2,0:T(8,128)}), f32[4,128,128]{1,2,0:T(8,128)}) %reduce-scatter.3.cloned.1.call-update) | async-done | bytes 262160 | tf_op jit(solution)/shard_map/reduce_scatter | solution.py:31
  169.2 1.0 sub.6
  170.2 0.1 copy.16
  170.3 46.9 %custom-call.7 = f32[4,128,128]{2,1,0:T(8,128)S(1)} custom-call(f32[4,128,128]{2,1,0:T(8,128)S(1)} %fusion.7), custom_call_target="Cholesky" | custom-call | tf_op jit(solution)/shard_map/jit(cholesky)/cholesky | solution.py:32
  217.3 0.1 compare_reduce_fusion
  217.4 0.8 select_bitcast_fusion
  218.2 39.3 %custom-call.8 = f32[4,1,128,128]{2,3,1,0:T(8,128)S(1)} custom-call(f32[4,1,128,128]{3,2,1,0:T(8,128)S(1)} %get-tuple-element.2), custom_call_target="InvertDiagBlocksLowerTriangular" | custom-call | tf_op jit(solution)/shard_map/triangular_solve | solution.py:34
  257.5 0.0 reduce-scatter.5.cloned.1.call-done
  257.5 0.0 copy-done.1
  257.6 1.0 sub.7
  258.5 1.3 fusion.5
  (5 shorter events, 0.1 us)
Async XLA Ops:
  7.2 104.2 %copy-start = (f32[256,128]{1,0:T(8,128)S(1)}, f32[256,128]{1,0:T(8,128)}, u32[]{:S(2)}) copy-start(f32[256,128]{1,0:T(8,128)} %param.5) | copy-start | bytes 393220
  7.2 82.0 %all-gather.2.cloned.1.call-start = ((), (), s32[]{:S(2)}) async-start(), calls=%async_computation.2 | async-start | bytes 8912896 | tf_op jit(solution)/shard_map/all_gather | solution.py:15
  7.9 161.3 %reduce-scatter.3.cloned.1.call-start = ((), (), s32[]{:S(2)}) async-start(), calls=%async_computation.3 | async-start | bytes 4456448 | tf_op jit(solution)/shard_map/reduce_scatter | solution.py:31
  105.9 151.7 %reduce-scatter.5.cloned.1.call-start = ((), (), s32[]{:S(2)}) async-start(), calls=%async_computation.4 | async-start | bytes 4456448 | tf_op jit(solution)/shard_map/reduce_scatter | solution.py:21
  111.3 12.2 %copy-start.2 = (f32[4,128,128]{2,1,0:T(8,128)S(1)}, f32[4,128,128]{2,1,0:T(8,128)}, u32[]{:S(2)}) copy-start(f32[4,128,128]{2,1,0:T(8,128)} %param.9) | copy-start | bytes 786436
  111.3 146.2 %copy-start.1 = (f32[512,128]{1,0:T(8,128)S(1)}, f32[512,128]{1,0:T(8,128)}, u32[]{:S(2)}) copy-start(f32[512,128]{1,0:T(8,128)} %param.8) | copy-start | bytes 786436
Sparse Core Ops, SparseCore 0:
  10.4 78.7 all-gather.1
  106.0 63.1 reduce-scatter.2
  171.7 62.2 reduce-scatter.4
where the time goes:
time: 267 us; the launch traced here: 266 us
  waiting for transfers between devices  126 us (47%)
  other arithmetic  89.9 us (34%)
  matrix products  30.1 us (11%)
  between operations  13.9 us (5%)
  local copies, waits for them, and re-layouts  5.94 us (2%)
    all_gather x1, waiting for transfers between devices, shards(): whole_pivot = lax.all_gather(pivot_rows, 'row', axis=0, tiled=True)  80.3 us
    another operation x4, other arithmetic, shards(): factor = jnp.linalg.cholesky(diag_in - dsum)  47.1 us
    reduce_scatter x1, waiting for transfers between devices, shards(): lax.psum_scatter(partial_diag, 'col', scatter_dimension=0, tiled=True)  45.4 us
    another operation x3, other arithmetic, shards(): lax.linalg.triangular_solve(factor, residue, left_side=True, lower=True)  40.1 us
    dot_general x1, matrix products, shards(): jnp.einsum('jak,jbk->jab', blocks, blocks, precision=lax.Precision.HIGHEST)  16.6 us
    dot_general x1, matrix products, shards(): jnp.dot(masked, lower_cols, precision=lax.Precision.HIGHEST, preferred_el...  12.2 us
    mul x2, local copies, waits for them, and re-layouts, shards(): whole_pivot.reshape(targets, B, k_local, B)  5.56 us
  transfers between devices with their start and end apart: 3, of which 2 were waited for; matrix products, arithmetic and copies ran while one was open for 40% of the time, Pallas kernels for 0%

commit v1 on v0

--- a/solution.py
+++ b/solution.py
@@ -12,7 +12,9 @@
     targets = pattern.shape[0]
     own_targets = diag_in.shape[0]
     width = panel_in.shape[1]
-    whole_pivot = lax.all_gather(pivot_rows, "row", axis=0, tiled=True)
+    whole_pivot = jnp.concatenate(
+        lax.all_to_all(jnp.stack([pivot_rows] * lax.axis_size("row")), "row", 0, 0), axis=0
+    )
     local_pattern = lax.dynamic_slice_in_dim(pattern, col_index * k_local, k_local, 1).astype(
         jnp.float32
     )

time: 267 us -> 350 us (1.31)
  waiting for transfers between devices: 126 us -> 197 us
  starting transfers between devices: 0.12 us -> 7.56 us
  local copies, waits for them, and re-layouts: 5.94 us -> 11 us
    all_to_all x0 -> x1, waiting for transfers between devices: none -> 104 us  [shards(): lax.all_to_all(jnp.stack([pivot_rows] * lax.axis_size('row')), 'row', 0, 0)]
    all_gather x1 -> x0, waiting for transfers between devices: 80.3 us -> none  [shards(): whole_pivot = lax.all_gather(pivot_rows, 'row', axis=0, tiled=True)]
    reduce_scatter x1, waiting for transfers between devices: 45.4 us -> 93.1 us  [shards(): lax.psum_scatter(partial_diag, 'col', scatter_dimension=0, tiled=True)]
    all_to_all x0 -> x1, starting transfers between devices: none -> 7.48 us  [shards(): lax.all_to_all(jnp.stack([pivot_rows] * lax.axis_size('row')), 'row', 0, 0)]
    another operation x0 -> x1, local copies, waits for them, and re-layouts: none -> 5.1 us  [shards(): jnp.stack([pivot_rows] * lax.axis_size('row'))]
  transfers between devices with their start and end apart: 3 -> 3, of which waited for: 2 -> 2; matrix products, arithmetic and copies ran while one was open for 40% -> 31% of each run, Pallas kernels for 0% -> 0%
where the time goes in v1:
time: 350 us
  waiting for transfers between devices  197 us (56%)
  other arithmetic  89.9 us (26%)
  matrix products  30.1 us (9%)
  between operations  14.1 us (4%)
  local copies, waits for them, and re-layouts  11 us (3%)
  starting transfers between devices  7.56 us (2%)
    all_to_all x1, waiting for transfers between devices, shards(): lax.all_to_all(jnp.stack([pivot_rows] * lax.axis_size('row')), 'row', 0, 0)  104 us
    reduce_scatter x1, waiting for transfers between devices, shards(): lax.psum_scatter(partial_diag, 'col', scatter_dimension=0, tiled=True)  93.1 us
    another operation x4, other arithmetic, shards(): factor = jnp.linalg.cholesky(diag_in - dsum)  47.1 us
    another operation x3, other arithmetic, shards(): lax.linalg.triangular_solve(factor, residue, left_side=True, lower=True)  40.1 us
    dot_general x1, matrix products, shards(): jnp.einsum('jak,jbk->jab', blocks, blocks, precision=lax.Precision.HIGHEST)  16.6 us
    dot_general x1, matrix products, shards(): jnp.dot(masked, lower_cols, precision=lax.Precision.HIGHEST, preferred_el...  12.2 us
    all_to_all x1, starting transfers between devices, shards(): lax.all_to_all(jnp.stack([pivot_rows] * lax.axis_size('row')), 'row', 0, 0)  7.48 us
  transfers between devices with their start and end apart: 3, of which 2 were waited for; matrix products, arithmetic and copies ran while one was open for 31% of the time, Pallas kernels for 0%

profile of v1, /device:TPU:2, one launch (start us, length us, event | category | flops | bytes accessed | tf_op | source)
XLA Modules:
  0.0 349.7 jit_solution(5366923718302260636)
XLA Ops:
  7.2 0.0 copy-start
  7.2 5.1 %stack.2 = f32[16,512,256]{2,1,0:T(8,128)} broadcast(f32[512,256]{1,0:T(8,128)} %param.6), dimensions={1,2} | broadcast | bytes 8912896 | tf_op jit(solution)/shard_map/stack | solution.py:16
  12.3 7.5 %all-to-all-start = ((f32[16,512,256]{2,1,0:T(8,128)}), f32[16,512,256]{2,1,0:T(8,128)}, u32[]{:S(2)}, u32[]{:S(2)}) async-start(f32[16,512,256]{2,1,0:T(8,128)} %stack.2), calls=%async_computation | async-start | bytes 16777216 | tf_op jit(solution)/shard_map/all_to_all | solution.py:16
  19.8 0.0 reduce-scatter.3.cloned.1.call-start
  19.8 0.7 dynamic-slice_convert_fusion
  20.5 0.1 copy.13
  20.6 0.1 mul.24
  20.7 103.8 %all-to-all-done = f32[16,512,256]{2,1,0:T(8,128)} async-done(((f32[16,512,256]{2,1,0:T(8,128)}), f32[16,512,256]{2,1,0:T(8,128)}, u32[]{:S(2)}, u32[]{:S(2)}) %all-to-all-start) | async-done | bytes 8388640 | tf_op jit(solution)/shard_map/all_to_all | solution.py:16
  124.6 16.6 %fusion.2 = f32[64,128,128]{1,2,0:T(8,128)} fusion(f32[64,128,256]{2,1,0:T(8,128)} %bitcast, f32[64,256]{1,0:T(8,128)S(1)} %bitcast.26), kind=kOutput, calls=%fused_computation.3 | convolution fusion | flops 3223322624 | bytes 12648448 | tf_op jit(solution)/shard_map/jak,jbk->jab/dot_general | solution.py:32
  141.2 0.0 reduce-scatter.3.cloned.1.call-update
  141.2 0.0 reduce-scatter.5.cloned.1.call-start
  141.3 5.4 %mul.28 = f32[64,128,2,128]{3,2,1,0:T(2,128)} broadcast(f32[64,2]{1,0:T(8,128)S(1)} %copy.13), dimensions={0,2} | broadcast | bytes 8389120 | tf_op jit(solution)/shard_map/mul | solution.py:21
  146.7 0.0 copy-done
  146.7 0.0 copy-start.2
  146.7 0.0 copy-start.1
  146.7 12.2 %fusion = f32[8192,128]{1,0:T(8,128)} fusion(f32[256,128]{1,0:T(8,128)S(1)} %copy-done, f32[8192,256]{1,0:T(8,128)} %bitcast.4, f32[1024,8,2,128]{3,2,1,0:T(2,128)} %bitcast.24), kind=kOutput, calls=%fused_computation.1 | convolution fusion | flops 3223322624 | bytes 21102592 | tf_op jit(solution)/shard_map/dot_general | solution.py:24
  158.9 0.0 reduce-scatter.5.cloned.1.call-update
  158.9 0.0 copy-done.2
  158.9 0.1 copy.15
  159.1 93.1 %reduce-scatter.3.cloned.1.call-done = f32[4,128,128]{1,2,0:T(8,128)} async-done(((f32[64,128,128]{1,2,0:T(8,128)}), f32[4,128,128]{1,2,0:T(8,128)}) %reduce-scatter.3.cloned.1.call-update) | async-done | bytes 262160 | tf_op jit(solution)/shard_map/reduce_scatter | solution.py:33
  252.2 1.0 sub.6
  253.2 0.1 copy.16
  253.4 46.9 %custom-call.7 = f32[4,128,128]{2,1,0:T(8,128)S(1)} custom-call(f32[4,128,128]{2,1,0:T(8,128)S(1)} %fusion.7), custom_call_target="Cholesky" | custom-call | tf_op jit(solution)/shard_map/jit(cholesky)/cholesky | solution.py:34
  300.3 0.1 compare_reduce_fusion
  300.4 0.8 select_bitcast_fusion
  301.3 39.3 %custom-call.8 = f32[4,1,128,128]{2,3,1,0:T(8,128)S(1)} custom-call(f32[4,1,128,128]{3,2,1,0:T(8,128)S(1)} %get-tuple-element.2), custom_call_target="InvertDiagBlocksLowerTriangular" | custom-call | tf_op jit(solution)/shard_map/triangular_solve | solution.py:36
  340.6 0.0 reduce-scatter.5.cloned.1.call-done
  340.6 0.0 copy-done.1
  340.6 1.0 sub.7
  341.6 1.3 fusion.5
  (5 shorter events, 0.1 us)
Async XLA Ops:
  7.2 139.5 %copy-start = (f32[256,128]{1,0:T(8,128)S(1)}, f32[256,128]{1,0:T(8,128)}, u32[]{:S(2)}) copy-start(f32[256,128]{1,0:T(8,128)} %param.5) | copy-start | bytes 393220
  12.3 112.3 %all-to-all-start = ((f32[16,512,256]{2,1,0:T(8,128)}), f32[16,512,256]{2,1,0:T(8,128)}, u32[]{:S(2)}, u32[]{:S(2)}) async-start(f32[16,512,256]{2,1,0:T(8,128)} %stack.2), calls=%async_computation | async-start | bytes 16777216 | tf_op jit(solution)/shard_map/all_to_all | solution.py:16
  19.8 232.5 %reduce-scatter.3.cloned.1.call-start = ((), (), s32[]{:S(2)}) async-start(), calls=%async_computation.3 | async-start | bytes 4456448 | tf_op jit(solution)/shard_map/reduce_scatter | solution.py:33
  141.2 199.4 %reduce-scatter.5.cloned.1.call-start = ((), (), s32[]{:S(2)}) async-start(), calls=%async_computation.4 | async-start | bytes 4456448 | tf_op jit(solution)/shard_map/reduce_scatter | solution.py:23
  146.7 12.2 %copy-start.2 = (f32[4,128,128]{2,1,0:T(8,128)S(1)}, f32[4,128,128]{2,1,0:T(8,128)}, u32[]{:S(2)}) copy-start(f32[4,128,128]{2,1,0:T(8,128)} %param.9) | copy-start | bytes 786436
  146.7 193.9 %copy-start.1 = (f32[512,128]{1,0:T(8,128)S(1)}, f32[512,128]{1,0:T(8,128)}, u32[]{:S(2)}) copy-start(f32[512,128]{1,0:T(8,128)} %param.8) | copy-start | bytes 786436
Sparse Core Ops, SparseCore 0:
  141.3 110.8 reduce-scatter.2
  254.8 62.3 reduce-scatter.4
